TPU v7x, 32 devices: a whole 2x2x4 slice. The times are simulated.
32 devices in a mesh: band: 4 (over z), dom: 8 (over y, x, core).
Axes of the slice: x: 2, y: 2, z: 4, core: 2. Of those that a mesh axis runs over, the one named last changes fastest.
Arguments:
- orbitals: float32 [64, 48, 48, 128], P('band', 'dom'), may hold values from -6 to 6
- occupation: float32 [64], P('band'), may hold values from 0.005 to 0.03
- dielectric: float32 [48, 48, 128], P('dom'), may hold values from 1 to 10
- core_density: float32 [48, 48, 128], P('dom'), may hold values from 0.05 to 0.5
- start_field: float32 [48, 48, 128], P('dom'), may hold values from -6 to 6
Outputs:
- potential: float32 [48, 48, 128], P('dom')
- filtered: float32 [64, 48, 48, 128], P('band', 'dom')
All inputs are finite; a program needn't handle non-finite values.
Results may differ from a plain program's by a relative error of at most 0.00002.
Values sent between devices are 32-bit elements; how exact they have to be, the bound alone decides.
A program may use at most 64 MiB of HBM per device.

v0:
```python
import functools

import jax
import jax.numpy as jnp
from jax import lax
from jax.experimental import pallas as pl
from jax.experimental.pallas import tpu as pltpu
from jax.sharding import PartitionSpec as P

ITERS = 4
DEGREE = 4


coeff_one = 1.5
coeff_two = -0.15
coeff_three = 1.0 / 90.0
coeff_zero = -49.0 / 18.0
center_value = 5.25
half_value = 4.75
slater = -0.9847450218426964


def padded_2(cells, sides, width):
    for axis, dim in sides:
        count = lax.axis_size(axis)
        ends = count - 1
        head = lax.slice_in_dim(cells, 0, width, axis=dim)
        tail = lax.slice_in_dim(cells, cells.shape[dim] - width, cells.shape[dim], axis=dim)
        cells = jnp.concatenate(
            [
                lax.ppermute(tail, axis, [(i, (i + 1) % count) for i in range(ends)]),
                cells,
                lax.ppermute(head, axis, [((i + 1) % count, i) for i in range(ends)]),
            ],
            axis=dim,
        )
    return cells


def laplace(padded):
    size_x = padded.shape[-3] - 6
    size_y = padded.shape[-2] - 6
    size_z = padded.shape[-1] - 6
    core = padded[..., 3 : 3 + size_x, 3 : 3 + size_y, 3 : 3 + size_z]
    total = 3.0 * coeff_zero * core
    for dist, weight in ((1, coeff_one), (2, coeff_two), (3, coeff_three)):
        along = padded[..., 3 + dist : 3 + dist + size_x, 3 : 3 + size_y, 3 : 3 + size_z]
        along = along + padded[..., 3 - dist : 3 - dist + size_x, 3 : 3 + size_y, 3 : 3 + size_z]
        along = along + padded[..., 3 : 3 + size_x, 3 + dist : 3 + dist + size_y, 3 : 3 + size_z]
        along = along + padded[..., 3 : 3 + size_x, 3 - dist : 3 - dist + size_y, 3 : 3 + size_z]
        along = along + padded[..., 3 : 3 + size_x, 3 : 3 + size_y, 3 + dist : 3 + dist + size_z]
        along = along + padded[..., 3 : 3 + size_x, 3 : 3 + size_y, 3 - dist : 3 - dist + size_z]
        total = total + weight * along
    return total


def face_weights(permit, padded):
    weights = (
        0.5 * (permit + padded[2:, 1:-1, 1:-1]),
        0.5 * (permit + padded[:-2, 1:-1, 1:-1]),
        0.5 * (permit + padded[1:-1, 2:, 1:-1]),
        0.5 * (permit + padded[1:-1, :-2, 1:-1]),
        0.5 * (permit + padded[1:-1, 1:-1, 2:]),
        0.5 * (permit + padded[1:-1, 1:-1, :-2]),
    )
    denominator = weights[0] + weights[1] + weights[2] + weights[3] + weights[4] + weights[5]
    return (weights, denominator)


def sweep(padded, weights, denominator, source):
    numerator = weights[0] * padded[2:, 1:-1, 1:-1] + weights[1] * padded[:-2, 1:-1, 1:-1]
    numerator = (
        numerator + weights[2] * padded[1:-1, 2:, 1:-1] + weights[3] * padded[1:-1, :-2, 1:-1]
    )
    numerator = (
        numerator + weights[4] * padded[1:-1, 1:-1, 2:] + weights[5] * padded[1:-1, 1:-1, :-2]
    )
    return (numerator + source) / denominator


def copies_rim(block):
    padded = padded_2(block, (("dom", 0),), 1)
    return jnp.pad(padded, ((0, 0), (1, 1), (1, 1)))


def apply_extended(padded_x, pot):
    padded = jnp.pad(padded_x, ((0, 0), (0, 0), (3, 3), (3, 3)))
    inner = padded_x[:, 3:-3]
    return -0.5 * laplace(padded) + pot[None] * inner


def local(orbitals, occupation, dielectric, core_density, start_field):
    partial_density = jnp.sum(occupation[:, None, None, None] * orbitals * orbitals, axis=0)
    density = lax.psum(partial_density, "band")
    permit_pad = padded_2(dielectric, (("dom", 0),), 1)
    permit_pad = jnp.pad(permit_pad, ((0, 0), (1, 1), (1, 1)))
    weights, denominator = face_weights(dielectric, permit_pad)
    source = 4.0 * density
    field = start_field
    for turn_index in range(ITERS):
        field = sweep(copies_rim(field), weights, denominator, source)
    potential = field + slater * jnp.cbrt(density + core_density)

    def hamil(block):
        padded = padded_2(block, (("dom", 1),), 3)
        return apply_extended(padded, potential)

    before = orbitals
    current = (hamil(orbitals) - center_value * orbitals) / half_value
    for turn_index in range(DEGREE - 1):
        nextone = 2.0 * (hamil(current) - center_value * current) / half_value - before
        before = current
        current = nextone
    return (potential, current)


MESH = pl.DeviceIdType.MESH
AHEAD = 5


def exchange(count_band, count_dom, refs_in, potential_ref, filtered_ref, scratch):
    orbitals_ref, occupation_ref, dielectric_ref, core_ref, start_ref = refs_in
    (
        orbs, own, part_in, side, other, acc, density, eps, field_a, field_b, weights, inverse,
        core, pot_own, strength, wave, wave_next, result, stripes, sums,
        load_sem, halo_send, halo_recv, in_send, in_recv, acc_send, acc_recv,
        side_send, side_recv, other_send, other_recv, relay_send,
        den_send, den_recv, pot_send, pot_recv, swap_send, swap_recv, pass_send, pass_recv, out_send, out_recv, end_sem,
    ) = scratch
    norb, planes, rows, lanes = orbitals_ref.shape
    per = norb // count_dom
    wide = 8
    reach = 3
    band = lax.axis_index("band")
    dom = lax.axis_index("dom")
    middle = count_band // 2
    in_left = band < middle
    toward = jnp.where(in_left, 1, -1)
    inner = band + toward
    outer = band - toward
    has_outer = jnp.logical_and(band > 0, band < count_band - 1)
    is_mid = jnp.logical_or(band == middle - 1, band == middle)
    has_left = dom > 0
    has_right = dom < count_dom - 1
    partner = dom + 1 - 2 * lax.rem(dom, 2)
    body = pl.ds(wide, rows)

    def peer(step):
        return lax.rem(dom + step, count_dom)

    def remote(src, dst, send, recv, **where):
        return pltpu.make_async_remote_copy(
            src_ref=src, dst_ref=dst, send_sem=send, recv_sem=recv, device_id=where, device_id_type=MESH
        )

    loads = [
        pltpu.make_async_copy(orbitals_ref, orbs, load_sem.at[0]),
        pltpu.make_async_copy(dielectric_ref, eps.at[pl.ds(ITERS, planes), body], load_sem.at[1]),
        pltpu.make_async_copy(start_ref, field_a.at[pl.ds(ITERS, planes), body], load_sem.at[2]),
        pltpu.make_async_copy(core_ref, core, load_sem.at[3]),
    ]
    for index in range(per):
        loads.append(
            pltpu.make_async_copy(
                orbitals_ref.at[dom * per + index],
                wave.at[index, pl.ds(reach + dom * planes, planes), body],
                load_sem.at[4 + index],
            )
        )
    for copy in loads:
        copy.start()

    barrier = pltpu.get_barrier_semaphore()
    for step in range(1, count_dom):
        pl.semaphore_signal(barrier, inc=1, device_id={"dom": peer(step)}, device_id_type=MESH)
    pl.semaphore_signal(barrier, inc=1, device_id={"band": inner}, device_id_type=MESH)
    pl.semaphore_signal(barrier, inc=1, device_id={"band": band + 1 - 2 * lax.rem(band, 2)}, device_id_type=MESH)

    @pl.when(has_outer)
    def _():
        pl.semaphore_signal(barrier, inc=1, device_id={"band": outer}, device_id_type=MESH)

    def clear_rows(ref, index):
        ref[index, :wide, :] = jnp.zeros((wide, lanes), jnp.float32)
        ref[index, wide + rows :, :] = jnp.zeros((wide, lanes), jnp.float32)

    def clear_plane(ref, index):
        ref[index] = jnp.zeros(ref.shape[1:], jnp.float32)

    extent = planes + 2 * ITERS

    @pl.loop(0, extent)
    def _(index):
        clear_rows(eps, index)
        clear_rows(field_a, index)
        clear_rows(field_b, index)

    @pl.when(jnp.logical_not(has_left))
    def _():
        for index in range(ITERS):
            eps[index, body, :] = jnp.zeros((rows, lanes), jnp.float32)
            field_a[index, body, :] = jnp.zeros((rows, lanes), jnp.float32)
        for index in range(ITERS - 1):
            density[index] = jnp.zeros((rows, lanes), jnp.float32)

    @pl.when(jnp.logical_not(has_right))
    def _():
        for index in range(ITERS):
            eps[ITERS + planes + index, body, :] = jnp.zeros((rows, lanes), jnp.float32)
            field_a[ITERS + planes + index, body, :] = jnp.zeros((rows, lanes), jnp.float32)
        for index in range(ITERS - 1):
            density[ITERS - 1 + planes + index] = jnp.zeros((rows, lanes), jnp.float32)

    tall = count_dom * planes
    waves = [wave.at[index] for index in range(per)]
    for ref in waves + [wave_next]:
        for index in range(reach):
            clear_plane(ref, index)
            clear_plane(ref, reach + tall + index)

        @pl.loop(reach, reach + tall)
        def _(index, ref=ref):
            clear_rows(ref, index)

    pl.semaphore_wait(barrier, count_dom + 1 + jnp.where(has_outer, 1, 0))

    def halo(source, target, index):
        right = remote(
            source.at[pl.ds(planes - ITERS, ITERS)], target.at[pl.ds(0, ITERS), body],
            halo_send.at[index], halo_recv.at[index], dom=dom + 1,
        )
        left = remote(
            source.at[pl.ds(0, ITERS)], target.at[pl.ds(ITERS + planes, ITERS), body],
            halo_send.at[index + 1], halo_recv.at[index + 1], dom=dom - 1,
        )
        return right, left

    halos = [halo(dielectric_ref, eps, 0), halo(start_ref, field_a, 2)]
    depth = ITERS - 1
    den_right = remote(
        density.at[pl.ds(planes, depth)], density.at[pl.ds(0, depth)],
        den_send.at[0], den_recv.at[0], dom=dom + 1,
    )
    den_left = remote(
        density.at[pl.ds(depth, depth)], density.at[pl.ds(depth + planes, depth)],
        den_send.at[1], den_recv.at[1], dom=dom - 1,
    )

    def sides(pairs, start):
        @pl.when(has_right)
        def _():
            for right, left in pairs:
                if start:
                    right.start()
                else:
                    right.wait_send()
                    left.wait_recv()

        @pl.when(has_left)
        def _():
            for right, left in pairs:
                if start:
                    left.start()
                else:
                    left.wait_send()
                    right.wait_recv()

    sides(halos, True)

    def incoming(index, step):
        return remote(
            orbitals_ref.at[peer(step) * per + index],
            wave.at[index, pl.ds(reach + dom * planes, planes), body],
            in_send.at[index, step], in_recv.at[index, step], dom=peer(step),
        )

    for step in range(1, 1 + AHEAD):
        incoming(0, step).start()

    loads[0].wait()

    @pl.loop(0, planes)
    def _(plane):
        total = jnp.zeros((rows, lanes), jnp.float32)
        for index in range(norb):
            cells = orbs[index, plane]
            total = total + occupation_ref[index] * cells * cells
        own[plane] = total

    def to_inner(plane):
        return remote(acc.at[plane], part_in.at[plane], acc_send.at[plane], acc_recv.at[plane], band=inner)

    def cross(plane):
        return remote(acc.at[plane], other.at[plane], other_send.at[plane], other_recv.at[plane], band=inner)

    def back(plane, source):
        return remote(source.at[plane], side.at[plane], side_send.at[plane], side_recv.at[plane], band=outer)

    def relay(plane):
        return remote(other.at[plane], other.at[plane], relay_send.at[plane], other_recv.at[plane], band=outer)

    @pl.loop(0, planes)
    def _(plane):
        @pl.when(has_outer)
        def _():
            to_inner(plane).wait_recv()
            acc[plane] = own[plane] + part_in[plane]

        @pl.when(jnp.logical_not(has_outer))
        def _():
            acc[plane] = own[plane]

        @pl.when(is_mid)
        def _():
            cross(plane).start()

            @pl.when(has_outer)
            def _():
                back(plane, acc).start()

        @pl.when(jnp.logical_not(is_mid))
        def _():
            to_inner(plane).start()

    loads[1].wait()
    loads[2].wait()
    loads[3].wait()
    sides(halos, False)
    lane = lax.broadcasted_iota(jnp.int32, (rows, lanes), 1)
    row = lax.broadcasted_iota(jnp.int32, (rows, lanes), 0)
    zero = jnp.zeros((rows, lanes), jnp.float32)

    @pl.loop(1, extent - 1)
    def _(index):
        here = eps[index, body, :]
        ahead = jnp.where(lane < lanes - 1, pltpu.roll(here, lanes - 1, 1), zero)
        behind = jnp.where(lane > 0, pltpu.roll(here, 1, 1), zero)
        faces = (
            0.5 * (here + eps[index + 1, body, :]),
            0.5 * (here + eps[index - 1, body, :]),
            0.5 * (here + eps[index, wide + 1 : wide + 1 + rows, :]),
            0.5 * (here + eps[index, wide - 1 : wide - 1 + rows, :]),
            0.5 * (here + ahead),
            0.5 * (here + behind),
        )
        denominator = faces[0] + faces[1] + faces[2] + faces[3] + faces[4] + faces[5]
        cell = dom * planes + index - ITERS
        inside = jnp.logical_and(cell >= 0, cell < tall)
        factor = jnp.where(inside, 1.0 / jnp.where(inside, denominator, 1.0), zero)
        inverse[index] = 4.0 * factor
        for face in range(4):
            weights[face, index] = faces[face] * factor
        weights[4, index] = jnp.where(lane < lanes - 1, faces[4] * factor, zero)
        weights[5, index] = jnp.where(lane > 0, faces[5] * factor, zero)

    @pl.loop(0, planes)
    def _(plane):
        @pl.when(jnp.logical_not(is_mid))
        def _():
            back(plane, side).wait_recv()

            @pl.when(has_outer)
            def _():
                back(plane, side).start()

        cross(plane).wait_recv()

        @pl.when(has_outer)
        def _():
            relay(plane).start()

        @pl.when(is_mid)
        def _():
            density[depth + plane] = acc[plane] + other[plane]

        @pl.when(jnp.logical_not(is_mid))
        def _():
            density[depth + plane] = side[plane] + other[plane]

    sides([(den_right, den_left)], True)
    for step in range(1 + AHEAD, count_dom):
        incoming(0, step).start()
    sides([(den_right, den_left)], False)

    before, after = field_a, field_b
    for turn in range(ITERS):
        @pl.loop(1 + turn, extent - 1 - turn)
        def _(index, before=before, after=after):
            here = before[index, body, :]
            total = density[index - 1] * inverse[index]
            total = total + (
                weights[0, index] * before[index + 1, body, :]
                + weights[1, index] * before[index - 1, body, :]
            )
            total = total + (
                weights[2, index] * before[index, wide + 1 : wide + 1 + rows, :]
                + weights[3, index] * before[index, wide - 1 : wide - 1 + rows, :]
            )
            total = total + (
                weights[4, index] * pltpu.roll(here, lanes - 1, 1)
                + weights[5, index] * pltpu.roll(here, 1, 1)
            )
            after[index, body, :] = total

        before, after = after, before
    final = before

    @pl.loop(0, planes)
    def _(plane):
        cells = density[depth + plane] + core[plane]
        root = jnp.exp(jnp.log(cells) * (1.0 / 3.0))
        root = root - (root - cells / (root * root)) * (1.0 / 3.0)
        pot = final[ITERS + plane, body, :] + slater * root
        pot_own[plane] = pot
        strength[dom * planes + plane] = (pot - (center_value + 1.5 * coeff_zero)) * (2.0 / half_value)

    mine = pl.ds(dom * planes, planes)
    chips = count_dom // 2
    half = planes // 2
    odd = lax.rem(band, 2)
    mate = band + 1 - 2 * odd

    def piece(step, which):
        return pl.ds(lax.rem(dom + count_dom - 2 * step, count_dom) * planes + which * half, half)

    def spread(step):
        if step == 0:
            return remote(
                strength.at[mine], strength.at[mine], pot_send.at[0], pot_recv.at[0], dom=partner
            )
        here = strength.at[piece(0, odd)]
        return remote(here, here, pot_send.at[step], pot_recv.at[step], dom=peer(2 * step))

    def swap(step):
        here = strength.at[piece(step, odd)]
        return remote(here, here, swap_send.at[step], swap_recv.at[step], band=mate)

    def hand(step, late):
        here = strength.at[piece(step, 1 - odd if late else odd)]
        return remote(here, here, pass_send.at[step, late], pass_recv.at[step, late], dom=partner)

    for step in range(1, chips):
        spread(step).start()
    spread(0).start()
    for index in range(1, per):
        for step in range(1, count_dom):
            incoming(index, step).start()
    keep = pltpu.make_async_copy(pot_own, potential_ref, end_sem.at[0])
    keep.start()
    for step in range(1, chips):
        spread(step).wait_recv()
        swap(step).start()
        hand(step, 0).start()
    for step in range(1, chips):
        swap(step).wait_recv()
        hand(step, 1).start()
    spread(0).wait_recv()
    for step in range(1, chips):
        hand(step, 0).wait_recv()
        hand(step, 1).wait_recv()

    gap = jnp.abs(
        lax.broadcasted_iota(jnp.int32, (2 * lanes, lanes), 0) % lanes
        - lax.broadcasted_iota(jnp.int32, (2 * lanes, lanes), 1)
    )
    weight = jnp.where(gap == 1, 135.0, jnp.where(gap == 2, -13.5, jnp.where(gap == 3, 1.0, 0.0)))
    stripes[...] = weight.astype(jnp.bfloat16)
    scale = -coeff_three / half_value

    def double_h(ref, base, plane):
        cells = ref[pl.ds(reach + base, planes), body, :].reshape(planes * rows, lanes)
        high = cells.astype(jnp.bfloat16)
        rest = cells - high.astype(jnp.float32)
        mid = rest.astype(jnp.bfloat16)
        low = (rest - mid.astype(jnp.float32)).astype(jnp.bfloat16)
        lines = jnp.dot(
            jnp.concatenate([high, mid], axis=1), stripes[...], preferred_element_type=jnp.float32
        ) + jnp.dot(low, stripes[:lanes], preferred_element_type=jnp.float32)
        sums[...] = lines.reshape(planes, rows, lanes)
        for local_plane in range(planes):
            at = base + local_plane
            here = ref[reach + at, body, :]

            def around(dist):
                along = ref[reach + at + dist, body, :] + ref[reach + at - dist, body, :]
                return along + (
                    ref[reach + at, wide + dist : wide + dist + rows, :]
                    + ref[reach + at, wide - dist : wide - dist + rows, :]
                )

            total = sums[local_plane] + around(3)
            total = total + 135.0 * around(1) - 13.5 * around(2)
            plane(at, strength[at] * here + scale * total)

    def outgoing(index, step):
        block = peer(step)
        return remote(
            result.at[index, pl.ds(block * planes, planes)],
            filtered_ref.at[dom * per + index],
            out_send.at[index, step], out_recv.at[index, step], dom=block,
        )

    for index in range(per):
        ref = waves[index]
        loads[4 + index].wait()
        for step in range(1, count_dom):
            incoming(index, step).wait_recv()

        @pl.loop(0, count_dom)
        def _(brick, ref=ref):
            def put(at, value):
                wave_next[reach + at, body, :] = 0.5 * value

            double_h(ref, brick * planes, put)

        first, second = ref, wave_next
        for turn in range(DEGREE - 2):
            @pl.loop(0, count_dom)
            def _(brick, first=first, second=second):
                def put(at, value):
                    first[reach + at, body, :] = value - first[reach + at, body, :]

                double_h(second, brick * planes, put)

            first, second = second, first

        for step in list(range(1, count_dom)) + [0]:
            def put(at, value):
                result[index, at] = value - first[reach + at, body, :]

            double_h(second, peer(step) * planes, put)

            if step:
                outgoing(index, step).start()
            else:
                pltpu.make_async_copy(
                    result.at[index, mine], filtered_ref.at[dom * per + index], end_sem.at[1 + index]
                ).start()

    for step in range(chips):
        spread(step).wait_send()
    for step in range(1, chips):
        swap(step).wait_send()
        hand(step, 0).wait_send()
        hand(step, 1).wait_send()
    for index in range(per):
        for step in range(1, count_dom):
            incoming(index, step).wait_send()

    @pl.loop(0, planes)
    def _(plane):
        @pl.when(is_mid)
        def _():
            cross(plane).wait_send()

        @pl.when(jnp.logical_not(is_mid))
        def _():
            to_inner(plane).wait_send()

        @pl.when(has_outer)
        def _():
            back(plane, acc).wait_send()
            relay(plane).wait_send()

    keep.wait()
    for index in range(per):
        pltpu.make_async_copy(
            result.at[index, mine], filtered_ref.at[dom * per + index], end_sem.at[1 + index]
        ).wait()
        for step in range(1, count_dom):
            outgoing(index, step).wait()


def fast(count_band, count_dom, orbitals, occupation, dielectric, core_density, start_field):
    norb, planes, rows, lanes = orbitals.shape
    per = norb // count_dom
    tall = count_dom * planes
    extent = planes + 2 * ITERS
    high = rows + 16
    chips = count_dom // 2

    def vmem(*shape):
        return pltpu.VMEM(shape, jnp.float32)

    def dma(*shape):
        return pltpu.SemaphoreType.DMA(shape)

    scratch = [
        vmem(norb, planes, rows, lanes),
        vmem(planes, rows, lanes),
        vmem(planes, rows, lanes),
        vmem(planes, rows, lanes),
        vmem(planes, rows, lanes),
        vmem(planes, rows, lanes),
        vmem(planes + 2 * (ITERS - 1), rows, lanes),
        vmem(extent, high, lanes),
        vmem(extent, high, lanes),
        vmem(extent, high, lanes),
        vmem(6, extent, rows, lanes),
        vmem(extent, rows, lanes),
        vmem(planes, rows, lanes),
        vmem(planes, rows, lanes),
        vmem(tall, rows, lanes),
        vmem(per, tall + 6, high, lanes),
        vmem(tall + 6, high, lanes),
        vmem(per, tall, rows, lanes),
        pltpu.VMEM((2 * lanes, lanes), jnp.bfloat16),
        vmem(planes, rows, lanes),
        dma(4 + per),
        dma(4), dma(4),
        dma(per, count_dom), dma(per, count_dom),
        dma(planes), dma(planes),
        dma(planes), dma(planes),
        dma(planes), dma(planes),
        dma(planes),
        dma(2), dma(2),
        dma(chips), dma(chips),
        dma(chips), dma(chips),
        dma(chips, 2), dma(chips, 2),
        dma(per, count_dom), dma(per, count_dom),
        dma(1 + per),
    ]

    def kernel(*refs):
        exchange(count_band, count_dom, refs[:5], refs[5], refs[6], refs[7:])

    hbm = pl.BlockSpec(memory_space=pl.ANY)
    return pl.pallas_call(
        kernel,
        out_shape=(
            jax.ShapeDtypeStruct((planes, rows, lanes), jnp.float32),
            jax.ShapeDtypeStruct(orbitals.shape, jnp.float32),
        ),
        in_specs=[hbm, pl.BlockSpec(memory_space=pltpu.SMEM), hbm, hbm, hbm],
        out_specs=(hbm, hbm),
        scratch_shapes=scratch,
        compiler_params=pltpu.CompilerParams(
            collective_id=0, has_side_effects=True, vmem_limit_bytes=63 * 1024 * 1024
        ),
        name="filter_whole",
    )(orbitals, occupation, dielectric, core_density, start_field)


def program(count_band, count_dom, *arrays):
    norb, planes, rows, lanes = arrays[0].shape
    suits = (
        norb % count_dom == 0
        and count_dom % 2 == 0
        and count_dom > 2
        and count_band % 2 == 0
        and planes >= ITERS
        and planes % 2 == 0
        and rows % 8 == 0
        and lanes == 128
    )
    if suits:
        return fast(count_band, count_dom, *arrays)
    return local(*arrays)


def solution(mesh):
    return jax.shard_map(
        functools.partial(program, mesh.shape["band"], mesh.shape["dom"]),
        mesh=mesh,
        in_specs=(
            P("band", "dom", None, None),
            P("band"),
            P("dom", None, None),
            P("dom", None, None),
            P("dom", None, None),
        ),
        out_specs=(P("dom", None, None), P("band", "dom", None, None)),
        check_vma=False,
    )
```

profile of v0, /device:TPU:11, one launch (start us, length us, event | category | flops | bytes accessed | tf_op | source)
XLA Modules:
  0.0 76.6 jit_solution(8604739023224127785)
XLA Ops:
  0.6 71.1 %filter_whole.1 = (f32[6,48,128]{2,1,0:T(8,128)}, f32[16,6,48,128]{3,2,1,0:T(8,128)}) custom-call(f32[16,6,48,128]{3,2,1,0:T(8,128)} %refs_0_.1, f32[16]{0:T(128)} %refs_1_.1, f32[6,48,128]{2,1,0:T(8,128)} %refs_2_.1, f32[6,48,128]{2,1,0:T(8,128)} %refs_3_.1, f32[6,48,128]{2,1,0:T(8,128)} %refs_4_.1), custom_call_target="tpu_custom_call" | custom-call | tf_op jit(solution)/shard_map/filter_whole/pallas_call | solution.py:628
  71.8 1.6 %copy.9 = f32[6,48,128]{2,1,0:T(8,128)} copy(f32[6,48,128]{2,1,0:T(8,128)} %get-tuple-element.4) | data formatting | bytes 294912
  73.4 3.2 %copy.10 = f32[16,6,48,128]{3,2,1,0:T(8,128)} copy(f32[16,6,48,128]{3,2,1,0:T(8,128)} %get-tuple-element.5) | data formatting | bytes 4718592
where the time goes:
time: 76.8 us; the launch traced here: 76.6 us
  Pallas kernels  71.1 us (93%)
  local copies, waits for them, and re-layouts  4.81 us (6%)
    pallas_call x1, Pallas kernels, fast(): pl.pallas_call(kernel, out_shape=(jax.ShapeDtypeStruct((planes, rows, lan...  71.1 us
    unnamed x2, local copies, waits for them, and re-layouts  4.81 us

commit v1 on v0

--- a/solution.py
+++ b/solution.py
@@ -115,15 +115,15 @@
 
 
 MESH = pl.DeviceIdType.MESH
-AHEAD = 5
+FEEDS = (5, 7, 7)
 
 
 def exchange(count_band, count_dom, refs_in, potential_ref, filtered_ref, scratch):
     orbitals_ref, occupation_ref, dielectric_ref, core_ref, start_ref = refs_in
     (
-        orbs, own, part_in, side, other, acc, density, eps, field_a, field_b, weights, inverse,
+        orbs, share, own, part_in, side, other, acc, density, eps, fields, weights, inverse,
         core, pot_own, strength, wave, wave_next, result, stripes, sums,
-        load_sem, halo_send, halo_recv, in_send, in_recv, acc_send, acc_recv,
+        load_sem, share_sem, halo_send, halo_recv, in_send, in_recv, acc_send, acc_recv,
         side_send, side_recv, other_send, other_recv, relay_send,
         den_send, den_recv, pot_send, pot_recv, swap_send, swap_recv, pass_send, pass_recv, out_send, out_recv, end_sem,
     ) = scratch
@@ -156,7 +156,7 @@
     loads = [
         pltpu.make_async_copy(orbitals_ref, orbs, load_sem.at[0]),
         pltpu.make_async_copy(dielectric_ref, eps.at[pl.ds(ITERS, planes), body], load_sem.at[1]),
-        pltpu.make_async_copy(start_ref, field_a.at[pl.ds(ITERS, planes), body], load_sem.at[2]),
+        pltpu.make_async_copy(start_ref, fields.at[0, pl.ds(ITERS, planes), body], load_sem.at[2]),
         pltpu.make_async_copy(core_ref, core, load_sem.at[3]),
     ]
     for index in range(per):
@@ -167,6 +167,8 @@
                 load_sem.at[4 + index],
             )
         )
+    shares = pltpu.make_async_copy(occupation_ref, share, share_sem.at[0])
+    shares.start()
     for copy in loads:
         copy.start()
 
@@ -192,14 +194,14 @@
     @pl.loop(0, extent)
     def _(index):
         clear_rows(eps, index)
-        clear_rows(field_a, index)
-        clear_rows(field_b, index)
+        for turn in range(ITERS):
+            clear_rows(fields.at[turn], index)
 
     @pl.when(jnp.logical_not(has_left))
     def _():
         for index in range(ITERS):
             eps[index, body, :] = jnp.zeros((rows, lanes), jnp.float32)
-            field_a[index, body, :] = jnp.zeros((rows, lanes), jnp.float32)
+            fields[0, index, body, :] = jnp.zeros((rows, lanes), jnp.float32)
         for index in range(ITERS - 1):
             density[index] = jnp.zeros((rows, lanes), jnp.float32)
 
@@ -207,13 +209,12 @@
     def _():
         for index in range(ITERS):
             eps[ITERS + planes + index, body, :] = jnp.zeros((rows, lanes), jnp.float32)
-            field_a[ITERS + planes + index, body, :] = jnp.zeros((rows, lanes), jnp.float32)
+            fields[0, ITERS + planes + index, body, :] = jnp.zeros((rows, lanes), jnp.float32)
         for index in range(ITERS - 1):
             density[ITERS - 1 + planes + index] = jnp.zeros((rows, lanes), jnp.float32)
 
     tall = count_dom * planes
-    waves = [wave.at[index] for index in range(per)]
-    for ref in waves + [wave_next]:
+    for ref in [stack.at[index] for stack in (wave, wave_next) for index in range(per)]:
         for index in range(reach):
             clear_plane(ref, index)
             clear_plane(ref, reach + tall + index)
@@ -235,16 +236,17 @@
         )
         return right, left
 
-    halos = [halo(dielectric_ref, eps, 0), halo(start_ref, field_a, 2)]
+    halos = [halo(dielectric_ref, eps, 0), halo(start_ref, fields.at[0], 2)]
     depth = ITERS - 1
-    den_right = remote(
-        density.at[pl.ds(planes, depth)], density.at[pl.ds(0, depth)],
-        den_send.at[0], den_recv.at[0], dom=dom + 1,
-    )
-    den_left = remote(
-        density.at[pl.ds(depth, depth)], density.at[pl.ds(depth + planes, depth)],
-        den_send.at[1], den_recv.at[1], dom=dom - 1,
-    )
+
+    def den(plane, right):
+        spot = plane - (planes - depth) if right else plane
+        here = density.at[depth + plane]
+        there = density.at[spot] if right else density.at[depth + planes + spot]
+        way = 0 if right else 1
+        return remote(
+            here, there, den_send.at[way, spot], den_recv.at[way, spot], dom=dom + 1 if right else dom - 1
+        )
 
     def sides(pairs, start):
         @pl.when(has_right)
@@ -274,53 +276,66 @@
             in_send.at[index, step], in_recv.at[index, step], dom=peer(step),
         )
 
-    for step in range(1, 1 + AHEAD):
-        incoming(0, step).start()
-
+    bulk = [(index, step) for index in range(per) for step in range(1, count_dom)]
+
+    def feed(start, stop):
+        for index, step in bulk[start:stop]:
+            incoming(index, step).start()
+
+    feed(0, FEEDS[0])
+    shares.wait()
     loads[0].wait()
+
+    def to_inner(plane):
+        return remote(acc.at[plane], part_in.at[plane], acc_send.at[plane], acc_recv.at[plane], band=inner)
+
+    def cross(plane):
+        return remote(acc.at[plane], other.at[plane], other_send.at[plane], other_recv.at[plane], band=inner)
+
+    def back(plane, source):
+        return remote(source.at[plane], side.at[plane], side_send.at[plane], side_recv.at[plane], band=outer)
+
+    def relay(plane):
+        return remote(other.at[plane], other.at[plane], relay_send.at[plane], other_recv.at[plane], band=outer)
 
     @pl.loop(0, planes)
     def _(plane):
         total = jnp.zeros((rows, lanes), jnp.float32)
         for index in range(norb):
             cells = orbs[index, plane]
-            total = total + occupation_ref[index] * cells * cells
-        own[plane] = total
-
-    def to_inner(plane):
-        return remote(acc.at[plane], part_in.at[plane], acc_send.at[plane], acc_recv.at[plane], band=inner)
-
-    def cross(plane):
-        return remote(acc.at[plane], other.at[plane], other_send.at[plane], other_recv.at[plane], band=inner)
-
-    def back(plane, source):
-        return remote(source.at[plane], side.at[plane], side_send.at[plane], side_recv.at[plane], band=outer)
-
-    def relay(plane):
-        return remote(other.at[plane], other.at[plane], relay_send.at[plane], other_recv.at[plane], band=outer)
-
-    @pl.loop(0, planes)
-    def _(plane):
+            total = total + share[index] * cells * cells
+
         @pl.when(has_outer)
         def _():
+            own[plane] = total
+
+        @pl.when(jnp.logical_not(has_outer))
+        def _():
+            acc[plane] = total
+
+            @pl.when(is_mid)
+            def _():
+                cross(plane).start()
+
+            @pl.when(jnp.logical_not(is_mid))
+            def _():
+                to_inner(plane).start()
+
+    @pl.when(has_outer)
+    def _():
+        @pl.loop(0, planes)
+        def _(plane):
             to_inner(plane).wait_recv()
             acc[plane] = own[plane] + part_in[plane]
 
-        @pl.when(jnp.logical_not(has_outer))
-        def _():
-            acc[plane] = own[plane]
-
-        @pl.when(is_mid)
-        def _():
-            cross(plane).start()
-
-            @pl.when(has_outer)
+            @pl.when(is_mid)
             def _():
+                cross(plane).start()
                 back(plane, acc).start()
 
-        @pl.when(jnp.logical_not(is_mid))
-        def _():
-            to_inner(plane).start()
+            @pl.when(jnp.logical_not(is_mid))
+            def _():
+                to_inner(plane).start()
 
     loads[1].wait()
     loads[2].wait()
@@ -377,40 +392,60 @@
         def _():
             density[depth + plane] = side[plane] + other[plane]
 
-    sides([(den_right, den_left)], True)
-    for step in range(1 + AHEAD, count_dom):
-        incoming(0, step).start()
-    sides([(den_right, den_left)], False)
-
-    before, after = field_a, field_b
-    for turn in range(ITERS):
-        @pl.loop(1 + turn, extent - 1 - turn)
-        def _(index, before=before, after=after):
-            here = before[index, body, :]
-            total = density[index - 1] * inverse[index]
-            total = total + (
-                weights[0, index] * before[index + 1, body, :]
-                + weights[1, index] * before[index - 1, body, :]
-            )
-            total = total + (
-                weights[2, index] * before[index, wide + 1 : wide + 1 + rows, :]
-                + weights[3, index] * before[index, wide - 1 : wide - 1 + rows, :]
-            )
-            total = total + (
-                weights[4, index] * pltpu.roll(here, lanes - 1, 1)
-                + weights[5, index] * pltpu.roll(here, 1, 1)
-            )
-            after[index, body, :] = total
-
-        before, after = after, before
-    final = before
-
-    @pl.loop(0, planes)
-    def _(plane):
+        @pl.when(jnp.logical_and(has_right, plane >= planes - depth))
+        def _():
+            den(plane, True).start()
+
+        @pl.when(jnp.logical_and(has_left, plane < depth))
+        def _():
+            den(plane, False).start()
+
+    feed(FEEDS[0], FEEDS[1])
+
+    def sweep_at(turn, index):
+        before, after = fields.at[turn], fields.at[turn + 1]
+        here = before[index, body, :]
+        total = density[index - 1] * inverse[index]
+        total = total + (
+            weights[0, index] * before[index + 1, body, :] + weights[1, index] * before[index - 1, body, :]
+        )
+        total = total + (
+            weights[2, index] * before[index, wide + 1 : wide + 1 + rows, :]
+            + weights[3, index] * before[index, wide - 1 : wide - 1 + rows, :]
+        )
+        total = total + (
+            weights[4, index] * pltpu.roll(here, lanes - 1, 1) + weights[5, index] * pltpu.roll(here, 1, 1)
+        )
+        after[index, body, :] = total
+
+    for turn in range(ITERS - 1):
+        for index in range(ITERS + turn, ITERS + planes - turn):
+            sweep_at(turn, index)
+
+    @pl.when(has_left)
+    def _():
+        for spot in range(depth):
+            den(planes - depth + spot, True).wait_recv()
+
+    for turn in range(ITERS - 1):
+        for index in range(1 + turn, 1 + turn + depth):
+            sweep_at(turn, index)
+
+    @pl.when(has_right)
+    def _():
+        for spot in range(depth):
+            den(spot, False).wait_recv()
+
+    for turn in range(ITERS - 1):
+        for index in range(extent - 1 - turn - depth, extent - 1 - turn):
+            sweep_at(turn, index)
+
+    def potential_at(plane):
+        sweep_at(ITERS - 1, ITERS + plane)
         cells = density[depth + plane] + core[plane]
         root = jnp.exp(jnp.log(cells) * (1.0 / 3.0))
         root = root - (root - cells / (root * root)) * (1.0 / 3.0)
-        pot = final[ITERS + plane, body, :] + slater * root
+        pot = fields[ITERS, ITERS + plane, body, :] + slater * root
         pot_own[plane] = pot
         strength[dom * planes + plane] = (pot - (center_value + 1.5 * coeff_zero)) * (2.0 / half_value)
 
@@ -439,25 +474,32 @@
         here = strength.at[piece(step, 1 - odd if late else odd)]
         return remote(here, here, pass_send.at[step, late], pass_recv.at[step, late], dom=partner)
 
-    for step in range(1, chips):
+    steps = range(chips - 1, 0, -1)
+
+    @pl.loop(0, half)
+    def _(plane):
+        potential_at(odd * half + plane)
+
+    for step in steps:
         spread(step).start()
+    feed(FEEDS[1], FEEDS[2])
+
+    @pl.loop(0, half)
+    def _(plane):
+        potential_at((1 - odd) * half + plane)
+
     spread(0).start()
-    for index in range(1, per):
-        for step in range(1, count_dom):
-            incoming(index, step).start()
+    feed(FEEDS[2], len(bulk))
     keep = pltpu.make_async_copy(pot_own, potential_ref, end_sem.at[0])
     keep.start()
-    for step in range(1, chips):
+    for step in steps:
         spread(step).wait_recv()
         swap(step).start()
         hand(step, 0).start()
-    for step in range(1, chips):
+    for step in steps:
         swap(step).wait_recv()
         hand(step, 1).start()
     spread(0).wait_recv()
-    for step in range(1, chips):
-        hand(step, 0).wait_recv()
-        hand(step, 1).wait_recv()
 
     gap = jnp.abs(
         lax.broadcasted_iota(jnp.int32, (2 * lanes, lanes), 0) % lanes
@@ -467,8 +509,13 @@
     stripes[...] = weight.astype(jnp.bfloat16)
     scale = -coeff_three / half_value
 
-    def double_h(ref, base, plane):
-        cells = ref[pl.ds(reach + base, planes), body, :].reshape(planes * rows, lanes)
+    units = tall // reach
+    parts = planes // reach
+    span = 2 * parts
+    origin = (dom // 2) * span
+
+    def double_h(level, ref, base, put):
+        cells = ref[pl.ds(reach + base, reach), body, :].reshape(reach * rows, lanes)
         high = cells.astype(jnp.bfloat16)
         rest = cells - high.astype(jnp.float32)
         mid = rest.astype(jnp.bfloat16)
@@ -476,8 +523,8 @@
         lines = jnp.dot(
             jnp.concatenate([high, mid], axis=1), stripes[...], preferred_element_type=jnp.float32
         ) + jnp.dot(low, stripes[:lanes], preferred_element_type=jnp.float32)
-        sums[...] = lines.reshape(planes, rows, lanes)
-        for local_plane in range(planes):
+        sums[level] = lines.reshape(reach, rows, lanes)
+        for local_plane in range(reach):
             at = base + local_plane
             here = ref[reach + at, body, :]
 
@@ -488,54 +535,73 @@
                     + ref[reach + at, wide - dist : wide - dist + rows, :]
                 )
 
-            total = sums[local_plane] + around(3)
+            total = sums[level, local_plane] + around(3)
             total = total + 135.0 * around(1) - 13.5 * around(2)
-            plane(at, strength[at] * here + scale * total)
-
-    def outgoing(index, step):
-        block = peer(step)
-        return remote(
-            result.at[index, pl.ds(block * planes, planes)],
-            filtered_ref.at[dom * per + index],
-            out_send.at[index, step], out_recv.at[index, step], dom=block,
-        )
-
-    for index in range(per):
-        ref = waves[index]
-        loads[4 + index].wait()
-        for step in range(1, count_dom):
-            incoming(index, step).wait_recv()
-
-        @pl.loop(0, count_dom)
-        def _(brick, ref=ref):
-            def put(at, value):
-                wave_next[reach + at, body, :] = 0.5 * value
-
-            double_h(ref, brick * planes, put)
-
-        first, second = ref, wave_next
-        for turn in range(DEGREE - 2):
-            @pl.loop(0, count_dom)
-            def _(brick, first=first, second=second):
+            put(at, strength[at] * here + scale * total)
+
+    def leave(index, unit):
+        block = unit // parts
+        step = lax.rem(block - dom + count_dom, count_dom)
+        part = lax.rem(unit, parts)
+        here = result.at[index, pl.ds(unit * reach, reach)]
+        there = filtered_ref.at[dom * per + index, pl.ds(part * reach, reach)]
+        away = remote(here, there, out_send.at[index, step, part], out_recv.at[index, step, part], dom=block)
+        return step, away, pltpu.make_async_copy(here, there, end_sem.at[1 + index * parts + part])
+
+    def advance(level, tick):
+        spot = tick - 2 * level
+
+        @pl.when(jnp.logical_and(spot >= 0, spot < per * units))
+        def _():
+            index = spot // units
+            unit = lax.rem(origin + spot + level, units)
+            even, odds = wave.at[index], wave_next.at[index]
+
+            if level == 0:
                 def put(at, value):
-                    first[reach + at, body, :] = value - first[reach + at, body, :]
-
-                double_h(second, brick * planes, put)
-
-            first, second = second, first
-
-        for step in list(range(1, count_dom)) + [0]:
-            def put(at, value):
-                result[index, at] = value - first[reach + at, body, :]
-
-            double_h(second, peer(step) * planes, put)
-
-            if step:
-                outgoing(index, step).start()
+                    odds[reach + at, body, :] = 0.5 * value
+            elif level < DEGREE - 1:
+                onto = even if level % 2 else odds
+
+                def put(at, value):
+                    onto[reach + at, body, :] = value - onto[reach + at, body, :]
             else:
-                pltpu.make_async_copy(
-                    result.at[index, mine], filtered_ref.at[dom * per + index], end_sem.at[1 + index]
-                ).start()
+                def put(at, value):
+                    result[index, at] = value - even[reach + at, body, :]
+
+            double_h(level, odds if level % 2 else even, unit * reach, put)
+            if level == DEGREE - 1:
+                step, away, home = leave(index, unit)
+
+                @pl.when(step > 0)
+                def _():
+                    away.start()
+
+                @pl.when(step == 0)
+                def _():
+                    home.start()
+
+    @pl.loop(0, per * units + 2 * (DEGREE - 1))
+    def _(tick):
+        @pl.when(jnp.logical_and(lax.rem(tick, units) == 0, tick < per * units))
+        def _():
+            index = tick // units
+            pltpu.make_async_copy(
+                orbitals_ref.at[dom * per + index],
+                wave.at[index, pl.ds(reach + dom * planes, planes), body],
+                load_sem.at[4 + index],
+            ).wait()
+            for step in range(1, count_dom):
+                incoming(index, step).wait_recv()
+
+        for turn in range(1, chips):
+            @pl.when(tick == turn * span)
+            def _(step=chips - turn):
+                hand(step, 0).wait_recv()
+                hand(step, 1).wait_recv()
+
+        for level in range(DEGREE):
+            advance(level, tick)
 
     for step in range(chips):
         spread(step).wait_send()
@@ -562,13 +628,41 @@
             back(plane, acc).wait_send()
             relay(plane).wait_send()
 
+        @pl.when(jnp.logical_and(has_right, plane >= planes - depth))
+        def _():
+            den(plane, True).wait_send()
+
+        @pl.when(jnp.logical_and(has_left, plane < depth))
+        def _():
+            den(plane, False).wait_send()
+
     keep.wait()
     for index in range(per):
-        pltpu.make_async_copy(
-            result.at[index, mine], filtered_ref.at[dom * per + index], end_sem.at[1 + index]
-        ).wait()
-        for step in range(1, count_dom):
-            outgoing(index, step).wait()
+        for part in range(parts):
+            leave(index, dom * parts + part)[2].wait()
+            for step in range(1, count_dom):
+                leave(index, peer(step) * parts + part)[1].wait()
+
+
+def deliver(direct, held_pot, held_filtered, potential_ref, filtered_ref, buf, pot_buf, in_sem, out_sem):
+    norb = held_filtered.shape[0]
+    if direct:
+        puts = [pltpu.make_async_copy(held_pot, potential_ref, out_sem.at[norb])]
+        puts += [pltpu.make_async_copy(held_filtered.at[i], filtered_ref.at[i], out_sem.at[i]) for i in range(norb)]
+        for put in puts:
+            put.start()
+    else:
+        gets = [pltpu.make_async_copy(held_pot, pot_buf, in_sem.at[norb])]
+        gets += [pltpu.make_async_copy(held_filtered.at[i], buf.at[i], in_sem.at[i]) for i in range(norb)]
+        puts = [pltpu.make_async_copy(pot_buf, potential_ref, out_sem.at[norb])]
+        puts += [pltpu.make_async_copy(buf.at[i], filtered_ref.at[i], out_sem.at[i]) for i in range(norb)]
+        for get in gets:
+            get.start()
+        for get, put in zip(gets, puts):
+            get.wait()
+            put.start()
+    for put in puts:
+        put.wait()
 
 
 def fast(count_band, count_dom, orbitals, occupation, dielectric, core_density, start_field):
@@ -585,8 +679,10 @@
     def dma(*shape):
         return pltpu.SemaphoreType.DMA(shape)
 
+    parts = planes // 3
     scratch = [
         vmem(norb, planes, rows, lanes),
+        pltpu.SMEM((norb,), jnp.float32),
         vmem(planes, rows, lanes),
         vmem(planes, rows, lanes),
         vmem(planes, rows, lanes),
@@ -594,51 +690,68 @@
         vmem(planes, rows, lanes),
         vmem(planes + 2 * (ITERS - 1), rows, lanes),
         vmem(extent, high, lanes),
-        vmem(extent, high, lanes),
-        vmem(extent, high, lanes),
+        vmem(ITERS + 1, extent, high, lanes),
         vmem(6, extent, rows, lanes),
         vmem(extent, rows, lanes),
         vmem(planes, rows, lanes),
         vmem(planes, rows, lanes),
         vmem(tall, rows, lanes),
         vmem(per, tall + 6, high, lanes),
-        vmem(tall + 6, high, lanes),
+        vmem(per, tall + 6, high, lanes),
         vmem(per, tall, rows, lanes),
         pltpu.VMEM((2 * lanes, lanes), jnp.bfloat16),
-        vmem(planes, rows, lanes),
+        vmem(DEGREE, 3, rows, lanes),
         dma(4 + per),
+        dma(1),
         dma(4), dma(4),
         dma(per, count_dom), dma(per, count_dom),
         dma(planes), dma(planes),
         dma(planes), dma(planes),
         dma(planes), dma(planes),
         dma(planes),
-        dma(2), dma(2),
+        dma(2, ITERS - 1), dma(2, ITERS - 1),
         dma(chips), dma(chips),
         dma(chips), dma(chips),
         dma(chips, 2), dma(chips, 2),
-        dma(per, count_dom), dma(per, count_dom),
-        dma(1 + per),
+        dma(per, count_dom, parts), dma(per, count_dom, parts),
+        dma(1 + per * parts),
     ]
 
     def kernel(*refs):
         exchange(count_band, count_dom, refs[:5], refs[5], refs[6], refs[7:])
 
     hbm = pl.BlockSpec(memory_space=pl.ANY)
-    return pl.pallas_call(
+
+    def pin(array):
+        return pltpu.with_memory_space_constraint(array, pltpu.HBM)
+
+    held = pl.pallas_call(
         kernel,
         out_shape=(
             jax.ShapeDtypeStruct((planes, rows, lanes), jnp.float32),
             jax.ShapeDtypeStruct(orbitals.shape, jnp.float32),
         ),
-        in_specs=[hbm, pl.BlockSpec(memory_space=pltpu.SMEM), hbm, hbm, hbm],
+        in_specs=[hbm] * 5,
         out_specs=(hbm, hbm),
         scratch_shapes=scratch,
         compiler_params=pltpu.CompilerParams(
-            collective_id=0, has_side_effects=True, vmem_limit_bytes=63 * 1024 * 1024
+            collective_id=0, has_side_effects=True, vmem_limit_bytes=40 * 1024 * 1024
         ),
         name="filter_whole",
-    )(orbitals, occupation, dielectric, core_density, start_field)
+    )(pin(orbitals), pin(occupation), pin(dielectric), pin(core_density), pin(start_field))
+    hold = (planes, rows, lanes) if not True else (8, 8, 128)
+    return pl.pallas_call(
+        functools.partial(deliver, True),
+        out_shape=(
+            jax.ShapeDtypeStruct((planes, rows, lanes), jnp.float32),
+            jax.ShapeDtypeStruct(orbitals.shape, jnp.float32),
+        ),
+        in_specs=[hbm, hbm],
+        out_specs=(hbm, hbm),
+        scratch_shapes=[vmem(norb, *hold), vmem(*hold), dma(norb + 1), dma(norb + 1)],
+        compiler_params=pltpu.CompilerParams(vmem_limit_bytes=16 * 1024 * 1024),
+        name="deliver",
+    )(*held)
 
 
 def program(count_band, count_dom, *arrays):
@@ -649,7 +762,7 @@
         and count_dom > 2
         and count_band % 2 == 0
         and planes >= ITERS
-        and planes % 2 == 0
+        and planes % 6 == 0
         and rows % 8 == 0
         and lanes == 128
     )

time: 76.8 us -> 69.7 us (0.908); the launches traced: 76.6 us -> 68.7 us
  local copies, waits for them, and re-layouts: 4.81 us -> 0 us
  Pallas kernels: 71.1 us -> 68.1 us
    pallas_call x1, Pallas kernels: 71.1 us -> 66.3 us  [fast(): pl.pallas_call(kernel, out_shape=(jax.ShapeDtypeStruct((planes, rows, lan...]
    unnamed x2 -> x0, local copies, waits for them, and re-layouts: 4.81 us -> none
    pallas_call x0 -> x1, Pallas kernels: none -> 1.74 us  [fast(): pl.pallas_call(functools.partial(deliver, True), out_shape=(jax.ShapeDtyp...]
where the time goes in v1:
time: 69.7 us; the launch traced here: 68.7 us
  Pallas kernels  68.1 us (98%)
    pallas_call x1, Pallas kernels, fast(): pl.pallas_call(kernel, out_shape=(jax.ShapeDtypeStruct((planes, rows, lan...  66.3 us
    pallas_call x1, Pallas kernels, fast(): pl.pallas_call(functools.partial(deliver, True), out_shape=(jax.ShapeDtyp...  1.74 us

profile of v1, /device:TPU:11, one launch (start us, length us, event | category | flops | bytes accessed | tf_op | source)
XLA Modules:
  0.0 68.7 jit_solution(6913377430589527583)
XLA Ops:
  0.6 66.3 %filter_whole.1 = (f32[6,48,128]{2,1,0:T(8,128)S(1)}, f32[16,6,48,128]{3,2,1,0:T(8,128)S(1)}) custom-call(f32[16,6,48,128]{3,2,1,0:T(8,128)} %refs_0_.1, f32[16]{0:T(128)} %refs_1_.1, f32[6,48,128]{2,1,0:T(8,128)} %refs_2_.1, f32[6,48,128]{2,1,0:T(8,128)} %refs_3_.1, f32[6,48,128]{2,1,0:T(8,128)} %refs_4_.1), custom_call_target="tpu_custom_call" | custom-call | tf_op jit(solution)/shard_map/filter_whole/pallas_call | solution.py:728
  66.9 1.7 %deliver.1 = (f32[6,48,128]{2,1,0:T(8,128)}, f32[16,6,48,128]{3,2,1,0:T(8,128)}) custom-call(f32[6,48,128]{2,1,0:T(8,128)S(1)} %get-tuple-element.4.held_pot, f32[16,6,48,128]{3,2,1,0:T(8,128)S(1)} %get-tuple-element.5.held_filtered), custom_call_target="tpu_custom_call" | custom-call | tf_op jit(solution)/shard_map/deliver/pallas_call | solution.py:743

commit v2 on v1

--- a/solution.py
+++ b/solution.py
@@ -115,18 +115,20 @@
 
 
 MESH = pl.DeviceIdType.MESH
-FEEDS = (5, 7, 7)
+FEEDS = (5, 7, 14)
+SWAP_AHEAD = 2
 
 
 def exchange(count_band, count_dom, refs_in, potential_ref, filtered_ref, scratch):
     orbitals_ref, occupation_ref, dielectric_ref, core_ref, start_ref = refs_in
     (
         orbs, share, own, part_in, side, other, acc, density, eps, fields, weights, inverse,
-        core, pot_own, strength, wave, wave_next, result, stripes, sums,
+        core, pot_own, strength, wave, later_one, later_two, later_three, result, stripes, sums,
         load_sem, share_sem, halo_send, halo_recv, in_send, in_recv, acc_send, acc_recv,
         side_send, side_recv, other_send, other_recv, relay_send,
-        den_send, den_recv, pot_send, pot_recv, swap_send, swap_recv, pass_send, pass_recv, out_send, out_recv, end_sem,
+        den_send, den_recv, pot_send, pot_recv, swap_send, swap_recv, mate_send, mate_recv, pass_send, pass_recv, out_send, out_recv, end_sem,
     ) = scratch
+    later = (later_one, later_two, later_three)
     norb, planes, rows, lanes = orbitals_ref.shape
     per = norb // count_dom
     wide = 8
@@ -144,6 +146,11 @@
     has_right = dom < count_dom - 1
     partner = dom + 1 - 2 * lax.rem(dom, 2)
     body = pl.ds(wide, rows)
+    half = planes // 2
+    chips = count_dom // 2
+    odd = lax.rem(band, 2)
+    mate = band + 1 - 2 * odd
+    shift = odd * half
 
     def peer(step):
         return lax.rem(dom + step, count_dom)
@@ -214,7 +221,7 @@
             density[ITERS - 1 + planes + index] = jnp.zeros((rows, lanes), jnp.float32)
 
     tall = count_dom * planes
-    for ref in [stack.at[index] for stack in (wave, wave_next) for index in range(per)]:
+    for ref in [stack.at[index] for stack in (wave, *later) for index in range(per)]:
         for index in range(reach):
             clear_plane(ref, index)
             clear_plane(ref, reach + tall + index)
@@ -223,20 +230,30 @@
         def _(index, ref=ref):
             clear_rows(ref, index)
 
+    gap = jnp.abs(
+        lax.broadcasted_iota(jnp.int32, (2 * lanes, lanes), 0) % lanes
+        - lax.broadcasted_iota(jnp.int32, (2 * lanes, lanes), 1)
+    )
+    weight = jnp.where(gap == 1, 135.0, jnp.where(gap == 2, -13.5, jnp.where(gap == 3, 1.0, 0.0)))
+    stripes[...] = weight.astype(jnp.bfloat16)
+    scale = -coeff_three / half_value
+
     pl.semaphore_wait(barrier, count_dom + 1 + jnp.where(has_outer, 1, 0))
 
-    def halo(source, target, index):
+    reserve = max(ITERS - half, 1)
+
+    def halo(source, target, index, deep_left):
+        from_left, from_right = (ITERS, reserve) if deep_left else (reserve, ITERS)
         right = remote(
-            source.at[pl.ds(planes - ITERS, ITERS)], target.at[pl.ds(0, ITERS), body],
+            source.at[pl.ds(planes - from_left, from_left)], target.at[pl.ds(ITERS - from_left, from_left), body],
             halo_send.at[index], halo_recv.at[index], dom=dom + 1,
         )
         left = remote(
-            source.at[pl.ds(0, ITERS)], target.at[pl.ds(ITERS + planes, ITERS), body],
+            source.at[pl.ds(0, from_right)], target.at[pl.ds(ITERS + planes, from_right), body],
             halo_send.at[index + 1], halo_recv.at[index + 1], dom=dom - 1,
         )
         return right, left
 
-    halos = [halo(dielectric_ref, eps, 0), halo(start_ref, fields.at[0], 2)]
     depth = ITERS - 1
 
     def den(plane, right):
@@ -248,26 +265,20 @@
             here, there, den_send.at[way, spot], den_recv.at[way, spot], dom=dom + 1 if right else dom - 1
         )
 
-    def sides(pairs, start):
-        @pl.when(has_right)
-        def _():
-            for right, left in pairs:
-                if start:
-                    right.start()
-                else:
-                    right.wait_send()
-                    left.wait_recv()
-
-        @pl.when(has_left)
-        def _():
-            for right, left in pairs:
-                if start:
-                    left.start()
-                else:
-                    left.wait_send()
-                    right.wait_recv()
-
-    sides(halos, True)
+    def sides(start):
+        for parity in range(2):
+            for here, mine, theirs in ((has_right, 0, 1), (has_left, 1, 0)):
+                @pl.when(jnp.logical_and(odd == parity, here))
+                def _(parity=parity, mine=mine, theirs=theirs):
+                    for source, target, index in ((dielectric_ref, eps, 0), (start_ref, fields.at[0], 2)):
+                        pair = halo(source, target, index, parity == 0)
+                        if start:
+                            pair[mine].start()
+                        else:
+                            pair[mine].wait_send()
+                            pair[theirs].wait_recv()
+
+    sides(True)
 
     def incoming(index, step):
         return remote(
@@ -282,7 +293,13 @@
         for index, step in bulk[start:stop]:
             incoming(index, step).start()
 
+    held = lax.rem(dom + band, 2) == 1
     feed(0, FEEDS[0])
+
+    @pl.when(jnp.logical_not(held))
+    def _():
+        feed(FEEDS[0], FEEDS[1])
+
     shares.wait()
     loads[0].wait()
 
@@ -337,36 +354,40 @@
             def _():
                 to_inner(plane).start()
 
-    loads[1].wait()
-    loads[2].wait()
-    loads[3].wait()
-    sides(halos, False)
-    lane = lax.broadcasted_iota(jnp.int32, (rows, lanes), 1)
-    row = lax.broadcasted_iota(jnp.int32, (rows, lanes), 0)
-    zero = jnp.zeros((rows, lanes), jnp.float32)
-
-    @pl.loop(1, extent - 1)
-    def _(index):
-        here = eps[index, body, :]
-        ahead = jnp.where(lane < lanes - 1, pltpu.roll(here, lanes - 1, 1), zero)
-        behind = jnp.where(lane > 0, pltpu.roll(here, 1, 1), zero)
-        faces = (
-            0.5 * (here + eps[index + 1, body, :]),
-            0.5 * (here + eps[index - 1, body, :]),
-            0.5 * (here + eps[index, wide + 1 : wide + 1 + rows, :]),
-            0.5 * (here + eps[index, wide - 1 : wide - 1 + rows, :]),
-            0.5 * (here + ahead),
-            0.5 * (here + behind),
-        )
-        denominator = faces[0] + faces[1] + faces[2] + faces[3] + faces[4] + faces[5]
-        cell = dom * planes + index - ITERS
-        inside = jnp.logical_and(cell >= 0, cell < tall)
-        factor = jnp.where(inside, 1.0 / jnp.where(inside, denominator, 1.0), zero)
-        inverse[index] = 4.0 * factor
-        for face in range(4):
-            weights[face, index] = faces[face] * factor
-        weights[4, index] = jnp.where(lane < lanes - 1, faces[4] * factor, zero)
-        weights[5, index] = jnp.where(lane > 0, faces[5] * factor, zero)
+    def settle():
+        loads[1].wait()
+        loads[2].wait()
+        loads[3].wait()
+        sides(False)
+        lane = lax.broadcasted_iota(jnp.int32, (rows, lanes), 1)
+        row = lax.broadcasted_iota(jnp.int32, (rows, lanes), 0)
+        zero = jnp.zeros((rows, lanes), jnp.float32)
+
+        @pl.loop(0, half + 2 * depth)
+        def _(spot):
+            index = 1 + shift + spot
+            here = eps[index, body, :]
+            ahead = jnp.where(lane < lanes - 1, pltpu.roll(here, lanes - 1, 1), zero)
+            behind = jnp.where(lane > 0, pltpu.roll(here, 1, 1), zero)
+            faces = (
+                0.5 * (here + eps[index + 1, body, :]),
+                0.5 * (here + eps[index - 1, body, :]),
+                0.5 * (here + eps[index, wide + 1 : wide + 1 + rows, :]),
+                0.5 * (here + eps[index, wide - 1 : wide - 1 + rows, :]),
+                0.5 * (here + ahead),
+                0.5 * (here + behind),
+            )
+            denominator = faces[0] + faces[1] + faces[2] + faces[3] + faces[4] + faces[5]
+            cell = dom * planes + index - ITERS
+            inside = jnp.logical_and(cell >= 0, cell < tall)
+            factor = jnp.where(inside, 1.0 / jnp.where(inside, denominator, 1.0), zero)
+            inverse[index] = 4.0 * factor
+            for face in range(4):
+                weights[face, index] = faces[face] * factor
+            weights[4, index] = jnp.where(lane < lanes - 1, faces[4] * factor, zero)
+            weights[5, index] = jnp.where(lane > 0, faces[5] * factor, zero)
+
+    pl.when(jnp.logical_not(is_mid))(settle)
 
     @pl.loop(0, planes)
     def _(plane):
@@ -392,15 +413,19 @@
         def _():
             density[depth + plane] = side[plane] + other[plane]
 
-        @pl.when(jnp.logical_and(has_right, plane >= planes - depth))
+        @pl.when(jnp.logical_and(jnp.logical_and(odd == 0, has_right), plane >= planes - depth))
         def _():
             den(plane, True).start()
 
-        @pl.when(jnp.logical_and(has_left, plane < depth))
+        @pl.when(jnp.logical_and(jnp.logical_and(odd == 1, has_left), plane < depth))
         def _():
             den(plane, False).start()
 
-    feed(FEEDS[0], FEEDS[1])
+    pl.when(is_mid)(settle)
+
+    @pl.when(held)
+    def _():
+        feed(FEEDS[0], FEEDS[1])
 
     def sweep_at(turn, index):
         before, after = fields.at[turn], fields.at[turn + 1]
@@ -419,26 +444,24 @@
         after[index, body, :] = total
 
     for turn in range(ITERS - 1):
-        for index in range(ITERS + turn, ITERS + planes - turn):
-            sweep_at(turn, index)
-
-    @pl.when(has_left)
+        first = turn + jnp.where(odd == 0, ITERS, 1 + half)
+        for spot in range(half + depth - 2 * turn):
+            sweep_at(turn, first + spot)
+
+    @pl.when(jnp.logical_and(odd == 0, has_left))
     def _():
         for spot in range(depth):
             den(planes - depth + spot, True).wait_recv()
 
-    for turn in range(ITERS - 1):
-        for index in range(1 + turn, 1 + turn + depth):
-            sweep_at(turn, index)
-
-    @pl.when(has_right)
+    @pl.when(jnp.logical_and(odd == 1, has_right))
     def _():
         for spot in range(depth):
             den(spot, False).wait_recv()
 
     for turn in range(ITERS - 1):
-        for index in range(extent - 1 - turn - depth, extent - 1 - turn):
-            sweep_at(turn, index)
+        first = jnp.where(odd == 0, 1 + turn, ITERS + planes - turn)
+        for spot in range(depth):
+            sweep_at(turn, first + spot)
 
     def potential_at(plane):
         sweep_at(ITERS - 1, ITERS + plane)
@@ -450,21 +473,21 @@
         strength[dom * planes + plane] = (pot - (center_value + 1.5 * coeff_zero)) * (2.0 / half_value)
 
     mine = pl.ds(dom * planes, planes)
-    chips = count_dom // 2
-    half = planes // 2
-    odd = lax.rem(band, 2)
-    mate = band + 1 - 2 * odd
 
     def piece(step, which):
         return pl.ds(lax.rem(dom + count_dom - 2 * step, count_dom) * planes + which * half, half)
 
+    near = jnp.where(lax.rem(dom // 2, 2) == 0, chips - 1, 1)
+    order = [near] + [2 * pair for pair in range(1, chips // 2)]
+    order += [lax.rem(near + 2 * pair, chips) for pair in range(1, chips // 2)]
+
     def spread(step):
-        if step == 0:
-            return remote(
-                strength.at[mine], strength.at[mine], pot_send.at[0], pot_recv.at[0], dom=partner
-            )
         here = strength.at[piece(0, odd)]
         return remote(here, here, pot_send.at[step], pot_recv.at[step], dom=peer(2 * step))
+
+    def share_pot():
+        here = pot_own.at[pl.ds(shift, half)]
+        return remote(here, here, mate_send.at[0], mate_recv.at[0], band=mate)
 
     def swap(step):
         here = strength.at[piece(step, odd)]
@@ -474,48 +497,51 @@
         here = strength.at[piece(step, 1 - odd if late else odd)]
         return remote(here, here, pass_send.at[step, late], pass_recv.at[step, late], dom=partner)
 
-    steps = range(chips - 1, 0, -1)
-
     @pl.loop(0, half)
-    def _(plane):
-        potential_at(odd * half + plane)
-
-    for step in steps:
-        spread(step).start()
+    def _(spot):
+        potential_at(shift + spot)
+
+    for step in order:
+        spread(chips - step).start()
+    swap(0).start()
+    hand(0, 0).start()
+    share_pot().start()
     feed(FEEDS[1], FEEDS[2])
 
-    @pl.loop(0, half)
-    def _(plane):
-        potential_at((1 - odd) * half + plane)
-
-    spread(0).start()
-    feed(FEEDS[2], len(bulk))
-    keep = pltpu.make_async_copy(pot_own, potential_ref, end_sem.at[0])
-    keep.start()
-    for step in steps:
+    def pass_on(step):
         spread(step).wait_recv()
         swap(step).start()
         hand(step, 0).start()
-    for step in steps:
-        swap(step).wait_recv()
-        hand(step, 1).start()
-    spread(0).wait_recv()
-
-    gap = jnp.abs(
-        lax.broadcasted_iota(jnp.int32, (2 * lanes, lanes), 0) % lanes
-        - lax.broadcasted_iota(jnp.int32, (2 * lanes, lanes), 1)
-    )
-    weight = jnp.where(gap == 1, 135.0, jnp.where(gap == 2, -13.5, jnp.where(gap == 3, 1.0, 0.0)))
-    stripes[...] = weight.astype(jnp.bfloat16)
-    scale = -coeff_three / half_value
+
+    for step in order[: chips // 2]:
+        pass_on(step)
+    swap(0).wait_recv()
+    hand(0, 1).start()
+    feed(FEEDS[2], len(bulk))
+    for step in order[chips // 2 :]:
+        pass_on(step)
 
     units = tall // reach
     parts = planes // reach
     span = 2 * parts
     origin = (dom // 2) * span
 
-    def double_h(level, ref, base, put):
-        cells = ref[pl.ds(reach + base, reach), body, :].reshape(reach * rows, lanes)
+    levels = (wave, *later)
+
+    def place(level, tick):
+        spot = jnp.maximum(tick - 3 * level, 0)
+        return jnp.minimum(spot // units, per - 1), lax.rem(origin + level + spot, units)
+
+    def advance(tick):
+        places = [place(level, tick) for level in range(DEGREE)]
+        sources = [levels[level].at[places[level][0]] for level in range(DEGREE)]
+        cells = jnp.concatenate(
+            [
+                sources[level][pl.ds(reach + places[level][1] * reach, reach), body, :].reshape(reach * rows, lanes)
+                for level in range(DEGREE)
+            ],
+            axis=0,
+        )
         high = cells.astype(jnp.bfloat16)
         rest = cells - high.astype(jnp.float32)
         mid = rest.astype(jnp.bfloat16)
@@ -523,21 +549,32 @@
         lines = jnp.dot(
             jnp.concatenate([high, mid], axis=1), stripes[...], preferred_element_type=jnp.float32
         ) + jnp.dot(low, stripes[:lanes], preferred_element_type=jnp.float32)
-        sums[level] = lines.reshape(reach, rows, lanes)
-        for local_plane in range(reach):
-            at = base + local_plane
-            here = ref[reach + at, body, :]
-
-            def around(dist):
-                along = ref[reach + at + dist, body, :] + ref[reach + at - dist, body, :]
-                return along + (
-                    ref[reach + at, wide + dist : wide + dist + rows, :]
-                    + ref[reach + at, wide - dist : wide - dist + rows, :]
-                )
-
-            total = sums[level, local_plane] + around(3)
-            total = total + 135.0 * around(1) - 13.5 * around(2)
-            put(at, strength[at] * here + scale * total)
+        sums[...] = lines.reshape(DEGREE, reach, rows, lanes)
+        for level in reversed(range(DEGREE)):
+            index, unit = places[level]
+            ref = sources[level]
+            for local_plane in range(reach):
+                at = unit * reach + local_plane
+                here = ref[reach + at, body, :]
+
+                def around(dist):
+                    along = ref[reach + at + dist, body, :] + ref[reach + at - dist, body, :]
+                    return along + (
+                        ref[reach + at, wide + dist : wide + dist + rows, :]
+                        + ref[reach + at, wide - dist : wide - dist + rows, :]
+                    )
+
+                total = sums[level, local_plane] + around(3)
+                total = total + 135.0 * around(1) - 13.5 * around(2)
+                value = strength[at] * here + scale * total
+                if level == 0:
+                    value = 0.5 * value
+                else:
+                    value = value - levels[level - 1][index, reach + at, body, :]
+                if level < DEGREE - 1:
+                    levels[level + 1][index, reach + at, body, :] = value
+                else:
+                    result[index, at] = value
 
     def leave(index, unit):
         block = unit // parts
@@ -548,40 +585,10 @@
         away = remote(here, there, out_send.at[index, step, part], out_recv.at[index, step, part], dom=block)
         return step, away, pltpu.make_async_copy(here, there, end_sem.at[1 + index * parts + part])
 
-    def advance(level, tick):
-        spot = tick - 2 * level
-
-        @pl.when(jnp.logical_and(spot >= 0, spot < per * units))
-        def _():
-            index = spot // units
-            unit = lax.rem(origin + spot + level, units)
-            even, odds = wave.at[index], wave_next.at[index]
-
-            if level == 0:
-                def put(at, value):
-                    odds[reach + at, body, :] = 0.5 * value
-            elif level < DEGREE - 1:
-                onto = even if level % 2 else odds
-
-                def put(at, value):
-                    onto[reach + at, body, :] = value - onto[reach + at, body, :]
-            else:
-                def put(at, value):
-                    result[index, at] = value - even[reach + at, body, :]
-
-            double_h(level, odds if level % 2 else even, unit * reach, put)
-            if level == DEGREE - 1:
-                step, away, home = leave(index, unit)
-
-                @pl.when(step > 0)
-                def _():
-                    away.start()
-
-                @pl.when(step == 0)
-                def _():
-                    home.start()
-
-    @pl.loop(0, per * units + 2 * (DEGREE - 1))
+    hand(0, 0).wait_recv()
+    hand(0, 1).wait_recv()
+
+    @pl.loop(0, per * units + 3 * (DEGREE - 1))
     def _(tick):
         @pl.when(jnp.logical_and(lax.rem(tick, units) == 0, tick < per * units))
         def _():
@@ -594,18 +601,37 @@
             for step in range(1, count_dom):
                 incoming(index, step).wait_recv()
 
-        for turn in range(1, chips):
-            @pl.when(tick == turn * span)
-            def _(step=chips - turn):
+        for ahead in range(1, chips):
+            @pl.when(tick == ahead * span - SWAP_AHEAD)
+            def _(step=chips - ahead):
+                swap(step).wait_recv()
+                hand(step, 1).start()
+
+            @pl.when(tick == ahead * span)
+            def _(step=chips - ahead):
                 hand(step, 0).wait_recv()
                 hand(step, 1).wait_recv()
 
-        for level in range(DEGREE):
-            advance(level, tick)
-
+        advance(tick)
+
+        @pl.when(tick >= 3 * (DEGREE - 1))
+        def _():
+            step, away, home = leave(*place(DEGREE - 1, tick))
+
+            @pl.when(step > 0)
+            def _():
+                away.start()
+
+            @pl.when(step == 0)
+            def _():
+                home.start()
+
+    share_pot().wait()
+    keep = pltpu.make_async_copy(pot_own, potential_ref, end_sem.at[0])
+    keep.start()
+    for step in range(1, chips):
+        spread(step).wait_send()
     for step in range(chips):
-        spread(step).wait_send()
-    for step in range(1, chips):
         swap(step).wait_send()
         hand(step, 0).wait_send()
         hand(step, 1).wait_send()
@@ -628,11 +654,11 @@
             back(plane, acc).wait_send()
             relay(plane).wait_send()
 
-        @pl.when(jnp.logical_and(has_right, plane >= planes - depth))
+        @pl.when(jnp.logical_and(jnp.logical_and(odd == 0, has_right), plane >= planes - depth))
         def _():
             den(plane, True).wait_send()
 
-        @pl.when(jnp.logical_and(has_left, plane < depth))
+        @pl.when(jnp.logical_and(jnp.logical_and(odd == 1, has_left), plane < depth))
         def _():
             den(plane, False).wait_send()
 
@@ -698,6 +724,8 @@
         vmem(tall, rows, lanes),
         vmem(per, tall + 6, high, lanes),
         vmem(per, tall + 6, high, lanes),
+        vmem(per, tall + 6, high, lanes),
+        vmem(per, tall + 6, high, lanes),
         vmem(per, tall, rows, lanes),
         pltpu.VMEM((2 * lanes, lanes), jnp.bfloat16),
         vmem(DEGREE, 3, rows, lanes),
@@ -712,6 +740,7 @@
         dma(2, ITERS - 1), dma(2, ITERS - 1),
         dma(chips), dma(chips),
         dma(chips), dma(chips),
+        dma(1), dma(1),
         dma(chips, 2), dma(chips, 2),
         dma(per, count_dom, parts), dma(per, count_dom, parts),
         dma(1 + per * parts),
@@ -758,7 +787,7 @@
     norb, planes, rows, lanes = arrays[0].shape
     suits = (
         norb % count_dom == 0
-        and count_dom % 2 == 0
+        and count_dom % 4 == 0
         and count_dom > 2
         and count_band % 2 == 0
         and planes >= ITERS

time: 69.7 us -> 67.7 us (0.971)
  Pallas kernels: 68.1 us -> 66.7 us
    pallas_call x1, Pallas kernels: 66.3 us -> 65 us  [fast(): pl.pallas_call(kernel, out_shape=(jax.ShapeDtypeStruct((planes, rows, lan...]
where the time goes in v2:
time: 67.7 us; the launch traced here: 67.3 us
  Pallas kernels  66.7 us (99%)
    pallas_call x1, Pallas kernels, fast(): pl.pallas_call(kernel, out_shape=(jax.ShapeDtypeStruct((planes, rows, lan...  65 us
    pallas_call x1, Pallas kernels, fast(): pl.pallas_call(functools.partial(deliver, True), out_shape=(jax.ShapeDtyp...  1.74 us

profile of v2, /device:TPU:11, one launch (start us, length us, event | category | flops | bytes accessed | tf_op | source)
XLA Modules:
  0.0 67.3 jit_solution(15483113090854019739)
XLA Ops:
  0.6 65.0 %filter_whole.1 = (f32[6,48,128]{2,1,0:T(8,128)S(1)}, f32[16,6,48,128]{3,2,1,0:T(8,128)S(1)}) custom-call(f32[16,6,48,128]{3,2,1,0:T(8,128)} %refs_0_.1, f32[16]{0:T(128)} %refs_1_.1, f32[6,48,128]{2,1,0:T(8,128)} %refs_2_.1, f32[6,48,128]{2,1,0:T(8,128)} %refs_3_.1, f32[6,48,128]{2,1,0:T(8,128)} %refs_4_.1), custom_call_target="tpu_custom_call" | custom-call | tf_op jit(solution)/shard_map/filter_whole/pallas_call | solution.py:757
  65.6 1.7 %deliver.1 = (f32[6,48,128]{2,1,0:T(8,128)}, f32[16,6,48,128]{3,2,1,0:T(8,128)}) custom-call(f32[6,48,128]{2,1,0:T(8,128)S(1)} %get-tuple-element.4.held_pot, f32[16,6,48,128]{3,2,1,0:T(8,128)S(1)} %get-tuple-element.5.held_filtered), custom_call_target="tpu_custom_call" | custom-call | tf_op jit(solution)/shard_map/deliver/pallas_call | solution.py:772

commit v3 on v2

--- a/solution.py
+++ b/solution.py
@@ -115,7 +115,7 @@
 
 
 MESH = pl.DeviceIdType.MESH
-FEEDS = (5, 7, 14)
+FEEDS = (5, 6, 14)
 SWAP_AHEAD = 2
 
 
@@ -197,47 +197,7 @@
         ref[index] = jnp.zeros(ref.shape[1:], jnp.float32)
 
     extent = planes + 2 * ITERS
-
-    @pl.loop(0, extent)
-    def _(index):
-        clear_rows(eps, index)
-        for turn in range(ITERS):
-            clear_rows(fields.at[turn], index)
-
-    @pl.when(jnp.logical_not(has_left))
-    def _():
-        for index in range(ITERS):
-            eps[index, body, :] = jnp.zeros((rows, lanes), jnp.float32)
-            fields[0, index, body, :] = jnp.zeros((rows, lanes), jnp.float32)
-        for index in range(ITERS - 1):
-            density[index] = jnp.zeros((rows, lanes), jnp.float32)
-
-    @pl.when(jnp.logical_not(has_right))
-    def _():
-        for index in range(ITERS):
-            eps[ITERS + planes + index, body, :] = jnp.zeros((rows, lanes), jnp.float32)
-            fields[0, ITERS + planes + index, body, :] = jnp.zeros((rows, lanes), jnp.float32)
-        for index in range(ITERS - 1):
-            density[ITERS - 1 + planes + index] = jnp.zeros((rows, lanes), jnp.float32)
-
     tall = count_dom * planes
-    for ref in [stack.at[index] for stack in (wave, *later) for index in range(per)]:
-        for index in range(reach):
-            clear_plane(ref, index)
-            clear_plane(ref, reach + tall + index)
-
-        @pl.loop(reach, reach + tall)
-        def _(index, ref=ref):
-            clear_rows(ref, index)
-
-    gap = jnp.abs(
-        lax.broadcasted_iota(jnp.int32, (2 * lanes, lanes), 0) % lanes
-        - lax.broadcasted_iota(jnp.int32, (2 * lanes, lanes), 1)
-    )
-    weight = jnp.where(gap == 1, 135.0, jnp.where(gap == 2, -13.5, jnp.where(gap == 3, 1.0, 0.0)))
-    stripes[...] = weight.astype(jnp.bfloat16)
-    scale = -coeff_three / half_value
-
     pl.semaphore_wait(barrier, count_dom + 1 + jnp.where(has_outer, 1, 0))
 
     reserve = max(ITERS - half, 1)
@@ -284,8 +244,12 @@
         return remote(
             orbitals_ref.at[peer(step) * per + index],
             wave.at[index, pl.ds(reach + dom * planes, planes), body],
-            in_send.at[index, step], in_recv.at[index, step], dom=peer(step),
-        )
+            in_send.at[index], in_recv.at[index], dom=peer(step),
+        )
+
+    def arrived(index, send, recv):
+        here = result.at[index, pl.ds(0, tall - planes)]
+        return remote(here, wave.at[index, pl.ds(reach, tall - planes), body], send.at[index], recv.at[index], dom=partner)
 
     bulk = [(index, step) for index in range(per) for step in range(1, count_dom)]
 
@@ -337,6 +301,46 @@
             @pl.when(jnp.logical_not(is_mid))
             def _():
                 to_inner(plane).start()
+
+
+    @pl.loop(0, extent)
+    def _(index):
+        clear_rows(eps, index)
+        for turn in range(ITERS):
+            clear_rows(fields.at[turn], index)
+
+    @pl.when(jnp.logical_not(has_left))
+    def _():
+        for index in range(ITERS):
+            eps[index, body, :] = jnp.zeros((rows, lanes), jnp.float32)
+            fields[0, index, body, :] = jnp.zeros((rows, lanes), jnp.float32)
+        for index in range(ITERS - 1):
+            density[index] = jnp.zeros((rows, lanes), jnp.float32)
+
+    @pl.when(jnp.logical_not(has_right))
+    def _():
+        for index in range(ITERS):
+            eps[ITERS + planes + index, body, :] = jnp.zeros((rows, lanes), jnp.float32)
+            fields[0, ITERS + planes + index, body, :] = jnp.zeros((rows, lanes), jnp.float32)
+        for index in range(ITERS - 1):
+            density[ITERS - 1 + planes + index] = jnp.zeros((rows, lanes), jnp.float32)
+
+    for ref in [stack.at[index] for stack in (wave, *later) for index in range(per)]:
+        for index in range(reach):
+            clear_plane(ref, index)
+            clear_plane(ref, reach + tall + index)
+
+        @pl.loop(reach, reach + tall)
+        def _(index, ref=ref):
+            clear_rows(ref, index)
+
+    gap = jnp.abs(
+        lax.broadcasted_iota(jnp.int32, (2 * lanes, lanes), 0) % lanes
+        - lax.broadcasted_iota(jnp.int32, (2 * lanes, lanes), 1)
+    )
+    weight = jnp.where(gap == 1, 135.0, jnp.where(gap == 2, -13.5, jnp.where(gap == 3, 1.0, 0.0)))
+    stripes[...] = weight.astype(jnp.bfloat16)
+    scale = -coeff_three / half_value
 
     @pl.when(has_outer)
     def _():
@@ -582,7 +586,7 @@
         part = lax.rem(unit, parts)
         here = result.at[index, pl.ds(unit * reach, reach)]
         there = filtered_ref.at[dom * per + index, pl.ds(part * reach, reach)]
-        away = remote(here, there, out_send.at[index, step, part], out_recv.at[index, step, part], dom=block)
+        away = remote(here, there, out_send.at[index], out_recv.at[index], dom=block)
         return step, away, pltpu.make_async_copy(here, there, end_sem.at[1 + index * parts + part])
 
     hand(0, 0).wait_recv()
@@ -598,8 +602,7 @@
                 wave.at[index, pl.ds(reach + dom * planes, planes), body],
                 load_sem.at[4 + index],
             ).wait()
-            for step in range(1, count_dom):
-                incoming(index, step).wait_recv()
+            arrived(index, in_send, in_recv).wait_recv()
 
         for ahead in range(1, chips):
             @pl.when(tick == ahead * span - SWAP_AHEAD)
@@ -636,8 +639,7 @@
         hand(step, 0).wait_send()
         hand(step, 1).wait_send()
     for index in range(per):
-        for step in range(1, count_dom):
-            incoming(index, step).wait_send()
+        arrived(index, in_send, in_recv).wait_send()
 
     @pl.loop(0, planes)
     def _(plane):
@@ -666,8 +668,7 @@
     for index in range(per):
         for part in range(parts):
             leave(index, dom * parts + part)[2].wait()
-            for step in range(1, count_dom):
-                leave(index, peer(step) * parts + part)[1].wait()
+        arrived(index, out_send, out_recv).wait()
 
 
 def deliver(direct, held_pot, held_filtered, potential_ref, filtered_ref, buf, pot_buf, in_sem, out_sem):
@@ -732,7 +733,7 @@
         dma(4 + per),
         dma(1),
         dma(4), dma(4),
-        dma(per, count_dom), dma(per, count_dom),
+        dma(per), dma(per),
         dma(planes), dma(planes),
         dma(planes), dma(planes),
         dma(planes), dma(planes),
@@ -742,7 +743,7 @@
         dma(chips), dma(chips),
         dma(1), dma(1),
         dma(chips, 2), dma(chips, 2),
-        dma(per, count_dom, parts), dma(per, count_dom, parts),
+        dma(per), dma(per),
         dma(1 + per * parts),
     ]
 

time: 67.7 us -> 65.9 us (0.973)
  Pallas kernels: 66.7 us -> 64.6 us
    pallas_call x1, Pallas kernels: 65 us -> 62.8 us  [fast(): pl.pallas_call(kernel, out_shape=(jax.ShapeDtypeStruct((planes, rows, lan...]
where the time goes in v3:
time: 65.9 us; the launch traced here: 65.2 us
  Pallas kernels  64.6 us (98%)
    pallas_call x1, Pallas kernels, fast(): pl.pallas_call(kernel, out_shape=(jax.ShapeDtypeStruct((planes, rows, lan...  62.8 us
    pallas_call x1, Pallas kernels, fast(): pl.pallas_call(functools.partial(deliver, True), out_shape=(jax.ShapeDtyp...  1.74 us

profile of v3, /device:TPU:11, one launch (start us, length us, event | category | flops | bytes accessed | tf_op | source)
XLA Modules:
  0.0 65.2 jit_solution(15237321809764209393)
XLA Ops:
  0.6 62.8 %filter_whole.1 = (f32[6,48,128]{2,1,0:T(8,128)S(1)}, f32[16,6,48,128]{3,2,1,0:T(8,128)S(1)}) custom-call(f32[16,6,48,128]{3,2,1,0:T(8,128)} %refs_0_.1, f32[16]{0:T(128)} %refs_1_.1, f32[6,48,128]{2,1,0:T(8,128)} %refs_2_.1, f32[6,48,128]{2,1,0:T(8,128)} %refs_3_.1, f32[6,48,128]{2,1,0:T(8,128)} %refs_4_.1), custom_call_target="tpu_custom_call" | custom-call | tf_op jit(solution)/shard_map/filter_whole/pallas_call | solution.py:758
  63.5 1.7 %deliver.1 = (f32[6,48,128]{2,1,0:T(8,128)}, f32[16,6,48,128]{3,2,1,0:T(8,128)}) custom-call(f32[6,48,128]{2,1,0:T(8,128)S(1)} %get-tuple-element.4.held_pot, f32[16,6,48,128]{3,2,1,0:T(8,128)S(1)} %get-tuple-element.5.held_filtered), custom_call_target="tpu_custom_call" | custom-call | tf_op jit(solution)/shard_map/deliver/pallas_call | solution.py:773

commit v4 on v3

--- a/solution.py
+++ b/solution.py
@@ -174,11 +174,6 @@
                 load_sem.at[4 + index],
             )
         )
-    shares = pltpu.make_async_copy(occupation_ref, share, share_sem.at[0])
-    shares.start()
-    for copy in loads:
-        copy.start()
-
     barrier = pltpu.get_barrier_semaphore()
     for step in range(1, count_dom):
         pl.semaphore_signal(barrier, inc=1, device_id={"dom": peer(step)}, device_id_type=MESH)
@@ -188,6 +183,11 @@
     @pl.when(has_outer)
     def _():
         pl.semaphore_signal(barrier, inc=1, device_id={"band": outer}, device_id_type=MESH)
+
+    shares = pltpu.make_async_copy(occupation_ref, share, share_sem.at[0])
+    shares.start()
+    for copy in loads:
+        copy.start()
 
     def clear_rows(ref, index):
         ref[index, :wide, :] = jnp.zeros((wide, lanes), jnp.float32)
@@ -222,7 +222,7 @@
         there = density.at[spot] if right else density.at[depth + planes + spot]
         way = 0 if right else 1
         return remote(
-            here, there, den_send.at[way, spot], den_recv.at[way, spot], dom=dom + 1 if right else dom - 1
+            here, there, den_send.at[way], den_recv.at[way, spot], dom=dom + 1 if right else dom - 1
         )
 
     def sides(start):
@@ -268,16 +268,16 @@
     loads[0].wait()
 
     def to_inner(plane):
-        return remote(acc.at[plane], part_in.at[plane], acc_send.at[plane], acc_recv.at[plane], band=inner)
+        return remote(acc.at[plane], part_in.at[plane], acc_send.at[0], acc_recv.at[plane], band=inner)
 
     def cross(plane):
-        return remote(acc.at[plane], other.at[plane], other_send.at[plane], other_recv.at[plane], band=inner)
+        return remote(acc.at[plane], other.at[plane], other_send.at[0], other_recv.at[plane], band=inner)
 
     def back(plane, source):
-        return remote(source.at[plane], side.at[plane], side_send.at[plane], side_recv.at[plane], band=outer)
+        return remote(source.at[plane], side.at[plane], side_send.at[0], side_recv.at[plane], band=outer)
 
     def relay(plane):
-        return remote(other.at[plane], other.at[plane], relay_send.at[plane], other_recv.at[plane], band=outer)
+        return remote(other.at[plane], other.at[plane], relay_send.at[0], other_recv.at[plane], band=outer)
 
     @pl.loop(0, planes)
     def _(plane):
@@ -487,7 +487,7 @@
 
     def spread(step):
         here = strength.at[piece(0, odd)]
-        return remote(here, here, pot_send.at[step], pot_recv.at[step], dom=peer(2 * step))
+        return remote(here, here, pot_send.at[0], pot_recv.at[step], dom=peer(2 * step))
 
     def share_pot():
         here = pot_own.at[pl.ds(shift, half)]
@@ -495,11 +495,11 @@
 
     def swap(step):
         here = strength.at[piece(step, odd)]
-        return remote(here, here, swap_send.at[step], swap_recv.at[step], band=mate)
+        return remote(here, here, swap_send.at[0], swap_recv.at[step], band=mate)
 
     def hand(step, late):
         here = strength.at[piece(step, 1 - odd if late else odd)]
-        return remote(here, here, pass_send.at[step, late], pass_recv.at[step, late], dom=partner)
+        return remote(here, here, pass_send.at[0], pass_recv.at[step, late], dom=partner)
 
     @pl.loop(0, half)
     def _(spot):
@@ -632,37 +632,35 @@
     share_pot().wait()
     keep = pltpu.make_async_copy(pot_own, potential_ref, end_sem.at[0])
     keep.start()
-    for step in range(1, chips):
-        spread(step).wait_send()
-    for step in range(chips):
-        swap(step).wait_send()
-        hand(step, 0).wait_send()
-        hand(step, 1).wait_send()
+    def gone(sent, send):
+        pltpu.make_async_copy(sent, sent, send).wait()
+
+    gone(strength.at[pl.ds(0, (chips - 1) * half)], pot_send.at[0])
+    gone(strength.at[pl.ds(0, chips * half)], swap_send.at[0])
+    gone(strength.at[pl.ds(0, chips * planes)], pass_send.at[0])
     for index in range(per):
         arrived(index, in_send, in_recv).wait_send()
 
-    @pl.loop(0, planes)
-    def _(plane):
-        @pl.when(is_mid)
-        def _():
-            cross(plane).wait_send()
-
-        @pl.when(jnp.logical_not(is_mid))
-        def _():
-            to_inner(plane).wait_send()
-
-        @pl.when(has_outer)
-        def _():
-            back(plane, acc).wait_send()
-            relay(plane).wait_send()
-
-        @pl.when(jnp.logical_and(jnp.logical_and(odd == 0, has_right), plane >= planes - depth))
-        def _():
-            den(plane, True).wait_send()
-
-        @pl.when(jnp.logical_and(jnp.logical_and(odd == 1, has_left), plane < depth))
-        def _():
-            den(plane, False).wait_send()
+    @pl.when(is_mid)
+    def _():
+        gone(acc, other_send.at[0])
+
+    @pl.when(jnp.logical_not(is_mid))
+    def _():
+        gone(acc, acc_send.at[0])
+
+    @pl.when(has_outer)
+    def _():
+        gone(acc, side_send.at[0])
+        gone(acc, relay_send.at[0])
+
+    @pl.when(jnp.logical_and(odd == 0, has_right))
+    def _():
+        gone(density.at[pl.ds(0, depth)], den_send.at[0])
+
+    @pl.when(jnp.logical_and(odd == 1, has_left))
+    def _():
+        gone(density.at[pl.ds(0, depth)], den_send.at[1])
 
     keep.wait()
     for index in range(per):
@@ -734,15 +732,15 @@
         dma(1),
         dma(4), dma(4),
         dma(per), dma(per),
-        dma(planes), dma(planes),
-        dma(planes), dma(planes),
-        dma(planes), dma(planes),
-        dma(planes),
-        dma(2, ITERS - 1), dma(2, ITERS - 1),
-        dma(chips), dma(chips),
-        dma(chips), dma(chips),
+        dma(1), dma(planes),
+        dma(1), dma(planes),
+        dma(1), dma(planes),
+        dma(1),
+        dma(2), dma(2, ITERS - 1),
+        dma(1), dma(chips),
+        dma(1), dma(chips),
         dma(1), dma(1),
-        dma(chips, 2), dma(chips, 2),
+        dma(1), dma(chips, 2),
         dma(per), dma(per),
         dma(1 + per * parts),
     ]

time: 65.9 us -> 65.6 us (level)
  no operation moved by 1% of the time
where the time goes in v4:
time: 65.6 us; the launch traced here: 64.9 us
  Pallas kernels  64.2 us (98%)
    pallas_call x1, Pallas kernels, fast(): pl.pallas_call(kernel, out_shape=(jax.ShapeDtypeStruct((planes, rows, lan...  62.5 us
    pallas_call x1, Pallas kernels, fast(): pl.pallas_call(functools.partial(deliver, True), out_shape=(jax.ShapeDtyp...  1.74 us

profile of v4, /device:TPU:11, one launch (start us, length us, event | category | flops | bytes accessed | tf_op | source)
XLA Modules:
  0.0 64.9 jit_solution(17368938033027646542)
XLA Ops:
  0.6 62.5 %filter_whole.1 = (f32[6,48,128]{2,1,0:T(8,128)S(1)}, f32[16,6,48,128]{3,2,1,0:T(8,128)S(1)}) custom-call(f32[16,6,48,128]{3,2,1,0:T(8,128)} %refs_0_.1, f32[16]{0:T(128)} %refs_1_.1, f32[6,48,128]{2,1,0:T(8,128)} %refs_2_.1, f32[6,48,128]{2,1,0:T(8,128)} %refs_3_.1, f32[6,48,128]{2,1,0:T(8,128)} %refs_4_.1), custom_call_target="tpu_custom_call" | custom-call | tf_op jit(solution)/shard_map/filter_whole/pallas_call | solution.py:756
  63.1 1.7 %deliver.1 = (f32[6,48,128]{2,1,0:T(8,128)}, f32[16,6,48,128]{3,2,1,0:T(8,128)}) custom-call(f32[6,48,128]{2,1,0:T(8,128)S(1)} %get-tuple-element.4.held_pot, f32[16,6,48,128]{3,2,1,0:T(8,128)S(1)} %get-tuple-element.5.held_filtered), custom_call_target="tpu_custom_call" | custom-call | tf_op jit(solution)/shard_map/deliver/pallas_call | solution.py:771

commit v5 on v4

--- a/solution.py
+++ b/solution.py
@@ -257,7 +257,7 @@
         for index, step in bulk[start:stop]:
             incoming(index, step).start()
 
-    held = lax.rem(dom + band, 2) == 1
+    held = jnp.logical_and(lax.rem(dom + band, 2) == 1, jnp.where(odd == 0, dom < count_dom - 1, dom > 0))
     feed(0, FEEDS[0])
 
     @pl.when(jnp.logical_not(held))

time: 65.6 us -> 65.6 us (level)
  no operation moved by 1% of the time
where the time goes in v5:
time: 65.6 us; the launch traced here: 64.9 us
  Pallas kernels  64.2 us (98%)
    pallas_call x1, Pallas kernels, fast(): pl.pallas_call(kernel, out_shape=(jax.ShapeDtypeStruct((planes, rows, lan...  62.5 us
    pallas_call x1, Pallas kernels, fast(): pl.pallas_call(functools.partial(deliver, True), out_shape=(jax.ShapeDtyp...  1.74 us

profile of v5, /device:TPU:11, one launch (start us, length us, event | category | flops | bytes accessed | tf_op | source)
XLA Modules:
  0.0 64.9 jit_solution(12503237204466315978)
XLA Ops:
  0.6 62.5 %filter_whole.1 = (f32[6,48,128]{2,1,0:T(8,128)S(1)}, f32[16,6,48,128]{3,2,1,0:T(8,128)S(1)}) custom-call(f32[16,6,48,128]{3,2,1,0:T(8,128)} %refs_0_.1, f32[16]{0:T(128)} %refs_1_.1, f32[6,48,128]{2,1,0:T(8,128)} %refs_2_.1, f32[6,48,128]{2,1,0:T(8,128)} %refs_3_.1, f32[6,48,128]{2,1,0:T(8,128)} %refs_4_.1), custom_call_target="tpu_custom_call" | custom-call | tf_op jit(solution)/shard_map/filter_whole/pallas_call | solution.py:756
  63.1 1.7 %deliver.1 = (f32[6,48,128]{2,1,0:T(8,128)}, f32[16,6,48,128]{3,2,1,0:T(8,128)}) custom-call(f32[6,48,128]{2,1,0:T(8,128)S(1)} %get-tuple-element.4.held_pot, f32[16,6,48,128]{3,2,1,0:T(8,128)S(1)} %get-tuple-element.5.held_filtered), custom_call_target="tpu_custom_call" | custom-call | tf_op jit(solution)/shard_map/deliver/pallas_call | solution.py:771
